TPU v7x, 256 devices: a whole 4x4x8 slice. The times are simulated.
256 devices in a mesh: seq: 32 (over z_lo, y, core), batch: 8 (over x, z_hi).
Axes of the slice: x: 4, y: 4, z: 8 (z_hi: 2, z_lo: 4; z = z_hi * 4 + z_lo), core: 2. Of those that a mesh axis runs over, the one named last changes fastest.
Arguments:
- coarse: bfloat16 [8, 8192, 1536], P('batch', 'seq'), may hold values from -6 to 6
- skip: bfloat16 [8, 16384, 1536], P('batch', 'seq'), may hold values from -6 to 6
- depth_kernel: float32 [3, 1536], replicated, may hold values from -3.5 to 3.5
- sep_weight: bfloat16 [1536, 1536], P('seq'), may hold values from -0.15625 to 0.15625
- sep_bias: float32 [1536], replicated, may hold values from -3 to 3
- head_weight: bfloat16 [1536, 3840], P(None, 'seq'), may hold values from -0.15625 to 0.15625
- head_bias: float32 [3840], replicated, may hold values from -4 to 4
- strand_pair: int32 [3840], replicated, may hold values from 0 to 3839, as said below
Outputs:
- preds: bfloat16 [8, 16384, 3840], P('batch', 'seq')
Inputs may be any that keep to these rules, and one draw needn't show every extreme that they name: strand_pair is a permutation with strand_pair[strand_pair[t]] == t; about half of the tracks are paired with another one.
All inputs are finite; a program needn't handle non-finite values.
Results may differ from a plain program's by a relative error of at most 0.0053.
Values may be sent and summed in bfloat16 or wider, within the bound.
A program may use at most 64 MiB of HBM per device.

v0:
```python
import jax
import jax.numpy as jnp
from jax import lax
from jax.sharding import PartitionSpec as P


def with_halo(cells, sides, width):
    for axis, dim in sides:
        count = lax.axis_size(axis)
        ends = count - 1
        head = lax.slice_in_dim(cells, 0, width, axis=dim)
        tail = lax.slice_in_dim(cells, cells.shape[dim] - width, cells.shape[dim], axis=dim)
        cells = jnp.concatenate(
            [
                lax.ppermute(tail, axis, [(i, (i + 1) % count) for i in range(ends)]),
                cells,
                lax.ppermute(head, axis, [((i + 1) % count, i) for i in range(ends)]),
            ],
            axis=dim,
        )
    return cells


def from_partner(block, axis, apart):
    count = lax.axis_size(axis)
    route = []
    for low in range(count):
        high = low | 1 << apart
        if high != low and high < count:
            route += [(low, high), (high, low)]
    return lax.ppermute(block, axis, route)


def mirror_blocks(payload):
    devices = lax.axis_size("seq")
    rows = payload.shape[0]
    spread = lax.all_to_all(payload, "seq", split_axis=1, concat_axis=0, tiled=True)
    width = spread.shape[1]
    flipped = spread.reshape(devices, rows, width)[::-1].reshape(devices * rows, width)
    return lax.all_to_all(flipped, "seq", split_axis=0, concat_axis=1, tiled=True)


def per_device(
    coarse, skip, depth_kernel, sep_weight, sep_bias, head_weight, head_bias, strand_pair
):
    upsampled = jnp.repeat(coarse[0].astype(jnp.float32), 2, axis=0)
    merged = (upsampled + skip[0]).astype(jnp.bfloat16)
    padded = with_halo(merged, (("seq", 0),), 1)
    depthwise = (
        depth_kernel[0] * padded[:-2]
        + depth_kernel[1] * padded[1:-1]
        + depth_kernel[2] * padded[2:]
    )
    depthwise = depthwise.astype(jnp.bfloat16)
    pointwise = jnp.dot(
        depthwise,
        lax.all_gather(sep_weight, "seq", axis=0, tiled=True),
        preferred_element_type=jnp.float32,
    )
    features = jax.nn.gelu(pointwise + sep_bias, approximate=True).astype(jnp.bfloat16)
    strand_bit = lax.axis_size("batch").bit_length() - 2
    logits = jnp.dot(
        features,
        lax.all_gather(head_weight, "seq", axis=1, tiled=True),
        preferred_element_type=jnp.float32,
    )
    logits = logits + head_bias
    own_head = jax.nn.softplus(logits).astype(jnp.bfloat16)
    outgoing = jnp.take(own_head, strand_pair, axis=1)[::-1]
    crossed = from_partner(outgoing, "batch", strand_bit)
    received = mirror_blocks(crossed)
    averaged = 0.5 * (own_head.astype(jnp.float32) + received.astype(jnp.float32))
    return averaged.astype(jnp.bfloat16)[None]


def solution(mesh):
    in_specs = (
        P("batch", "seq", None),
        P("batch", "seq", None),
        P(),
        P("seq", None),
        P(),
        P(None, "seq"),
        P(),
        P(),
    )
    out_specs = P("batch", "seq", None)
    return jax.shard_map(
        per_device, mesh=mesh, in_specs=in_specs, out_specs=out_specs, check_vma=False
    )
```

profile of v0, /device:TPU:1, one launch (start us, length us, event | category | flops | bytes accessed | tf_op | source)
XLA Modules:
  0.0 566.6 jit_solution(9465348246911856683)
XLA Ops:
  6.5 0.0 all-gather.3.cloned.1.call-start
  6.5 0.7 all-gather.3.cloned.1.call-update
  7.3 0.0 all-gather.5.cloned.1.call-start
  7.3 0.7 all-gather.5.cloned.1.call-update
  8.0 1.3 bitcast_convert_fusion
  9.3 1.1 broadcast_in_dim.20
  10.4 3.3 reshape.28
  13.7 0.0 copy-start.1
  13.7 0.0 copy-start
  13.7 0.0 copy-start.2
  13.7 0.0 copy-start.3
  13.8 2.9 fusion.9
  16.6 4.6 collective-permute-start
  21.2 2.1 collective-permute-start.1
  23.3 0.0 copy-done.1
  23.3 0.1 slice_reduce_fusion.2
  23.4 0.0 copy-done
  23.5 0.0 collective-permute-done
  23.5 2.7 collective-permute-done.1
  26.2 50.3 %all-gather.3.cloned.1.call-done = bf16[1536,1536]{1,0:T(8,128)(2,1)} async-done(((bf16[48,1536]{1,0:T(8,128)(2,1)}), bf16[1536,1536]{1,0:T(8,128)(2,1)}) %all-gather.3.cloned.1.call-update) | async-done | bytes 4718608 | tf_op jit(solution)/shard_map/all_gather | solution.py:57
  76.5 76.9 %all-gather.5.cloned.1.call-done = bf16[1536,3840]{0,1:T(8,128)(2,1)} async-done(((bf16[1536,120]{0,1:T(8,128)(2,1)}), bf16[1536,3840]{0,1:T(8,128)(2,1)}) %all-gather.5.cloned.1.call-update) | async-done | bytes 11796496 | tf_op jit(solution)/shard_map/all_gather | solution.py:64
  153.4 0.0 copy-done.2
  153.4 0.0 copy-done.3
  153.4 19.8 %fusion = bf16[512,3840]{1,0:T(8,128)(2,1)} fusion(bf16[1536,3840]{0,1:T(8,128)(2,1)} %all-gather.5.cloned.1.call-done, f32[3840]{0:T(1024)S(1)} %copy-done.2, bf16[1536,1536]{1,0:T(8,128)(2,1)} %all-gather.3.cloned.1.call-done, bf16[512,1536]{1,0:T(8,128)(2,1)S(1)} %fusion.9, bf16[1,1536]{1,0:T(2,128)(2,1)S(1)} %collective-permute-done.1, ...), kind=kOutput, calls=%fused_computation.2 | convolution fusion | flops 8491106304 | bytes 22066176 | tf_op jit(solution)/shard_map/dot_general | solution.py:62
  173.2 6.3 %copy.11 = bf16[512,3840]{0,1:T(8,128)(2,1)} copy(bf16[512,3840]{1,0:T(8,128)(2,1)} %fusion) | data formatting | bytes 7864320 | tf_op jit(solution)/shard_map/convert_element_type | solution.py:68
  179.5 14.5 %gather_fusion = bf16[3840,512]{1,0:T(8,128)(2,1)} fusion(bf16[512,3840]{0,1:T(8,128)(2,1)} %copy.11, s32[4096]{0:T(1024)S(1)} %pad_clamp_fusion), kind=kCustom, calls=%fused_computation | custom fusion | bytes 7879680 | tf_op jit(solution)/shard_map/jit(_take)/gather | solution.py:69
  194.0 4.7 select_bitcast_fusion
  198.7 58.9 %rev.4 = bf16[512,3840]{0,1:T(8,128)(2,1)} reverse(bf16[512,3840]{0,1:T(8,128)(2,1)} %select_bitcast_fusion), dimensions={0} | reverse | bytes 7864320 | tf_op jit(solution)/shard_map/rev | solution.py:69
  257.7 2.7 collective-permute-start.2
  260.4 85.2 %collective-permute-done.2 = bf16[512,3840]{0,1:T(8,128)(2,1)S(1)} collective-permute-done((bf16[512,3840]{0,1:T(8,128)(2,1)}, bf16[512,3840]{0,1:T(8,128)(2,1)S(1)}, u32[]{:S(2)}, u32[]{:S(2)}) %collective-permute-start.2) | collective-permute-done | bytes 3932192 | tf_op jit(solution)/shard_map/ppermute | solution.py:31
  345.6 95.8 %all_to_all.29 = bf16[512,32,120]{0,2,1:T(8,128)(2,1)} all-to-all(bf16[512,32,120]{0,2,1:T(8,128)(2,1)S(1)} %bitcast.19), channel_id=1, replica_groups=mesh['seq'=32,'batch'=8] {'seq'}, dimensions={1} | all-to-all | bytes 7864320 | tf_op jit(solution)/shard_map/all_to_all | solution.py:37
  441.4 4.3 all_to_all.25
  445.7 93.5 %all_to_all.30 = bf16[32,512,120]{1,2,0:T(8,128)(2,1)S(1)} all-to-all(bf16[32,512,120]{1,2,0:T(8,128)(2,1)} %all_to_all.25), channel_id=1, replica_groups=mesh['seq'=32,'batch'=8] {'seq'}, dimensions={0} | all-to-all | bytes 7864320 | tf_op jit(solution)/shard_map/all_to_all | solution.py:40
  539.3 4.2 convert_element_type.67
  543.4 9.1 %copy.12 = f32[512,3840]{1,0:T(8,128)} copy(f32[512,3840]{0,1:T(8,128)} %bitcast.17) | data formatting | bytes 15728640 | tf_op jit(solution)/shard_map/convert_element_type | solution.py:72
  552.6 7.2 %fusion.1 = bf16[1,512,3840]{2,1,0:T(8,128)(2,1)} fusion(f32[512,3840]{1,0:T(8,128)} %copy.12, bf16[512,3840]{1,0:T(8,128)(2,1)} %fusion), kind=kLoop, calls=%fused_computation.5 | loop fusion | flops 7864320 | bytes 15728640 | tf_op jit(solution)/shard_map/broadcast_in_dim | solution.py:73
  (4 shorter events, 0.0 us)
Async XLA Ops:
  6.5 69.9 %all-gather.3.cloned.1.call-start = ((), (), s32[]{:S(2)}) async-start(), calls=%async_computation.2 | async-start | bytes 4866048 | tf_op jit(solution)/shard_map/all_gather | solution.py:57
  7.3 146.1 %all-gather.5.cloned.1.call-start = ((), (), s32[]{:S(2)}) async-start(), calls=%async_computation.3 | async-start | bytes 12165120 | tf_op jit(solution)/shard_map/all_gather | solution.py:64
  13.7 9.6 %copy-start.1 = (f32[3,1536]{1,0:T(4,128)S(1)}, f32[3,1536]{1,0:T(4,128)}, u32[]{:S(2)}) copy-start(f32[3,1536]{1,0:T(4,128)} %param.10) | copy-start | bytes 55300
  13.7 9.7 %copy-start = (s32[3840]{0:T(1024)S(1)}, s32[3840]{0:T(1024)}, u32[]{:S(2)}) copy-start(s32[3840]{0:T(1024)} %param.15) | copy-start | bytes 46084
  13.7 139.6 %copy-start.2 = (f32[3840]{0:T(1024)S(1)}, f32[3840]{0:T(1024)}, u32[]{:S(2)}) copy-start(f32[3840]{0:T(1024)} %param.14) | copy-start | bytes 46084
  13.7 139.6 %copy-start.3 = (f32[1536]{0:T(1024)S(1)}, f32[1536]{0:T(1024)}, u32[]{:S(2)}) copy-start(f32[1536]{0:T(1024)} %param.12) | copy-start | bytes 18436
  16.6 6.8 %collective-permute-start = (bf16[1,1536]{1,0:T(2,128)(2,1)S(1)}, bf16[1,1536]{1,0:T(2,128)(2,1)S(1)}, u32[]{:S(2)}, u32[]{:S(2)}) collective-permute-start(bf16[1,1536]{1,0:T(2,128)(2,1)S(1)} %get-tuple-element.8), channel_id=1, source_target_pairs={{0,8},{8,16},{16,24},{24,32},{32,40},{40,48},{48,56},{56,64},{64,7... | collective-permute-start | bytes 9224 | tf_op jit(solution)/shard_map/ppermute | solution.py:15
  21.2 4.9 collective-permute-start.1
  257.7 87.9 %collective-permute-start.2 = (bf16[512,3840]{0,1:T(8,128)(2,1)}, bf16[512,3840]{0,1:T(8,128)(2,1)S(1)}, u32[]{:S(2)}, u32[]{:S(2)}) collective-permute-start(bf16[512,3840]{0,1:T(8,128)(2,1)} %rev.4), channel_id=1, source_target_pairs={{0,4},{4,0},{1,5},{5,1},{2,6},{6,2},{3,7},{7,3},{8,12},{12,8},{9,1... | collective-permute-start | bytes 11796488 | tf_op jit(solution)/shard_map/ppermute | solution.py:31
Sparse Core Ops, SparseCore 0:
  9.2 67.2 all-gather.2
  78.3 75.0 all-gather.4
where the time goes:
time: 574 us; the launch traced here: 567 us
  waiting for transfers between devices  217 us (38%)
  blocking collectives  189 us (33%)
  local copies, waits for them, and re-layouts  97.6 us (17%)
  other arithmetic  20.3 us (4%)
  matrix products  19.8 us (3%)
  between operations  13.5 us (2%)
  starting transfers between devices  9.44 us (2%)
    all_to_all x1, blocking collectives, mirror_blocks(): lax.all_to_all(payload, 'seq', split_axis=1, concat_axis=0, tiled=True)  95.8 us
    all_to_all x1, blocking collectives, mirror_blocks(): lax.all_to_all(flipped, 'seq', split_axis=0, concat_axis=1, tiled=True)  93.5 us
    ppermute x1, waiting for transfers between devices, from_partner(): return lax.ppermute(block, axis, route)  85.2 us
    all_gather x1, waiting for transfers between devices, per_device(): lax.all_gather(head_weight, 'seq', axis=1, tiled=True)  76.9 us
    rev x1, local copies, waits for them, and re-layouts, per_device(): outgoing = jnp.take(own_head, strand_pair, axis=1)[::-1]  58.9 us
    all_gather x1, waiting for transfers between devices, per_device(): lax.all_gather(sep_weight, 'seq', axis=0, tiled=True)  50.3 us
    dot_general x1, matrix products, per_device(): jnp.dot(features, lax.all_gather(head_weight, 'seq', axis=1, tiled=True),...  19.8 us
    gather x1, local copies, waits for them, and re-layouts, per_device(): outgoing = jnp.take(own_head, strand_pair, axis=1)[::-1]  14.5 us
  transfers between devices with their start and end apart: 5, of which 4 were waited for; matrix products, arithmetic and copies ran while one was open for 2% of the time, Pallas kernels for 0%

commit v1 on v0

v1 whole, which is shorter than its diff:
```python
import jax
import jax.numpy as jnp
from jax import lax
from jax.sharding import PartitionSpec as P


def with_halo(cells, axis, width):
    count = lax.axis_size(axis)
    ends = count - 1
    head = lax.slice_in_dim(cells, 0, width, axis=0)
    tail = lax.slice_in_dim(cells, cells.shape[0] - width, cells.shape[0], axis=0)
    return jnp.concatenate(
        [
            lax.ppermute(tail, axis, [(i, (i + 1) % count) for i in range(ends)]),
            cells,
            lax.ppermute(head, axis, [((i + 1) % count, i) for i in range(ends)]),
        ],
        axis=0,
    )


def reversed_rows(x):
    rows = x.shape[0]
    r = lax.broadcasted_iota(jnp.int32, (rows, rows), 0)
    c = lax.broadcasted_iota(jnp.int32, (rows, rows), 1)
    flip = (r + c == rows - 1).astype(x.dtype)
    return jnp.dot(flip, x, preferred_element_type=jnp.float32).astype(x.dtype)


def to_mirror(x):
    nb, ns = lax.axis_size("batch"), lax.axis_size("seq")
    half = nb // 2
    route = []
    for s in range(ns):
        for b in range(nb):
            mirror = (ns - 1 - s) * nb + (b + half) % nb
            route.append((s * nb + b, mirror))
    return lax.ppermute(x, ("seq", "batch"), route)


def per_device(
    coarse, skip, depth_kernel, sep_weight, sep_bias, head_weight, head_bias, strand_pair
):
    sep_full = lax.all_gather(sep_weight, "seq", axis=0, tiled=True)
    head_full = lax.all_gather(head_weight, "seq", axis=1, tiled=True)
    upsampled = jnp.repeat(coarse[0].astype(jnp.float32), 2, axis=0)
    merged = (upsampled + skip[0]).astype(jnp.bfloat16)
    padded = with_halo(merged, "seq", 1)
    depthwise = (
        depth_kernel[0] * padded[:-2]
        + depth_kernel[1] * padded[1:-1]
        + depth_kernel[2] * padded[2:]
    )
    depthwise = depthwise.astype(jnp.bfloat16)
    mirrored = to_mirror(reversed_rows(depthwise))

    def head(block):
        pointwise = jnp.dot(block, sep_full, preferred_element_type=jnp.float32)
        features = jax.nn.gelu(pointwise + sep_bias, approximate=True).astype(jnp.bfloat16)
        logits = jnp.dot(features, head_full, preferred_element_type=jnp.float32)
        return jax.nn.softplus(logits + head_bias).astype(jnp.bfloat16)

    own = head(depthwise)
    other = jnp.take(head(mirrored), strand_pair, axis=1)
    averaged = 0.5 * (own.astype(jnp.float32) + other.astype(jnp.float32))
    return averaged.astype(jnp.bfloat16)[None]


def solution(mesh):
    in_specs = (
        P("batch", "seq", None),
        P("batch", "seq", None),
        P(),
        P("seq", None),
        P(),
        P(None, "seq"),
        P(),
        P(),
    )
    return jax.shard_map(
        per_device,
        mesh=mesh,
        in_specs=in_specs,
        out_specs=P("batch", "seq", None),
        check_vma=False,
    )
```

time: 574 us -> 286 us (0.50); the launches traced: 567 us -> 286 us
  blocking collectives: 189 us -> 0 us
  local copies, waits for them, and re-layouts: 97.6 us -> 31.5 us
  waiting for transfers between devices: 217 us -> 178 us
  matrix products: 19.8 us -> 44 us
  other arithmetic: 20.3 us -> 4.14 us
    all_to_all x2 -> x0, blocking collectives: 189 us -> none  [the longest x1 95.8 us: mirror_blocks(): lax.all_to_all(payload, 'seq', split_axis=1, concat_axis=0, tiled=True)]
    rev x1 -> x0, local copies, waits for them, and re-layouts: 58.9 us -> none  [per_device(): outgoing = jnp.take(own_head, strand_pair, axis=1)[::-1]]
    ppermute x1, waiting for transfers between devices: 85.2 us -> 39.6 us  [to_mirror(): return lax.ppermute(x, ('seq', 'batch'), route)]
    dot_general x1 -> x4, matrix products: 19.8 us -> 44 us  [the longest x2 35.8 us: head(): logits = jnp.dot(features, head_full, preferred_element_type=jnp.float32)]
    convert_element_type x2 -> x1, local copies, waits for them, and re-layouts: 15.4 us -> 6.29 us  [head(): return jax.nn.softplus(logits + head_bias).astype(jnp.bfloat16)]
    broadcast_in_dim x1 -> x0, other arithmetic: 7.17 us -> none  [per_device(): return averaged.astype(jnp.bfloat16)[None]]
    all_gather x2, waiting for transfers between devices: 127 us -> 134 us  [the longest x1 70 us: per_device(): head_full = lax.all_gather(head_weight, 'seq', axis=1, tiled=True)]
    gather x1 -> x2, local copies, waits for them, and re-layouts: 14.5 us -> 20.7 us  [per_device(): other = jnp.take(head(mirrored), strand_pair, axis=1)]
  transfers between devices with their start and end apart: 5 -> 5, of which waited for: 4 -> 4; matrix products, arithmetic and copies ran while one was open for 2% -> 6% of each run, Pallas kernels for 0% -> 0%
where the time goes in v1:
time: 286 us
  waiting for transfers between devices  178 us (62%)
  matrix products  44 us (15%)
  local copies, waits for them, and re-layouts  31.5 us (11%)
  starting transfers between devices  14.8 us (5%)
  between operations  13.5 us (5%)
  other arithmetic  4.14 us (1%)
    all_gather x1, waiting for transfers between devices, per_device(): head_full = lax.all_gather(head_weight, 'seq', axis=1, tiled=True)  70 us
    all_gather x1, waiting for transfers between devices, per_device(): sep_full = lax.all_gather(sep_weight, 'seq', axis=0, tiled=True)  64 us
    ppermute x1, waiting for transfers between devices, to_mirror(): return lax.ppermute(x, ('seq', 'batch'), route)  39.6 us
    dot_general x2, matrix products, head(): logits = jnp.dot(features, head_full, preferred_element_type=jnp.float32)  35.8 us
    gather x2, local copies, waits for them, and re-layouts, per_device(): other = jnp.take(head(mirrored), strand_pair, axis=1)  20.7 us
    ppermute x1, starting transfers between devices, to_mirror(): return lax.ppermute(x, ('seq', 'batch'), route)  8.27 us
    dot_general x1, matrix products, head(): pointwise = jnp.dot(block, sep_full, preferred_element_type=jnp.float32)  6.6 us
    convert_element_type x1, local copies, waits for them, and re-layouts, head(): return jax.nn.softplus(logits + head_bias).astype(jnp.bfloat16)  6.29 us
  transfers between devices with their start and end apart: 5, of which 4 were waited for; matrix products, arithmetic and copies ran while one was open for 6% of the time, Pallas kernels for 0%

profile of v1, /device:TPU:1, one launch (start us, length us, event | category | flops | bytes accessed | tf_op | source)
XLA Modules:
  0.0 285.9 jit_solution(13165414521046507312)
XLA Ops:
  6.5 0.0 all-gather.3.cloned.1.call-start
  6.5 0.7 all-gather.3.cloned.1.call-update
  7.3 0.0 all-gather.5.cloned.1.call-start
  7.3 0.7 all-gather.5.cloned.1.call-update
  8.0 1.3 bitcast_convert_fusion
  9.3 1.1 broadcast_in_dim.22
  10.4 3.3 %reshape.14 = f32[512,1536]{1,0:T(8,128)} reshape(f32[256,2,1536]{2,1,0:T(2,128)S(1)} %broadcast_in_dim.22) | data formatting | bytes 6291456 | tf_op jit(solution)/shard_map/reshape | solution.py:46
  13.7 0.0 copy-start.1
  13.7 2.8 fusion.19
  16.6 4.6 %collective-permute-start = (bf16[1,1536]{1,0:T(2,128)(2,1)S(1)}, bf16[1,1536]{1,0:T(2,128)(2,1)S(1)}, u32[]{:S(2)}, u32[]{:S(2)}) collective-permute-start(bf16[1,1536]{1,0:T(2,128)(2,1)S(1)} %get-tuple-element.8), channel_id=1, source_target_pairs={{0,8},{8,16},{16,24},{24,32},{32,40},{40,48},{48,56},{56,64},{64,7... | collective-permute-start | bytes 9224 | tf_op jit(solution)/shard_map/ppermute | solution.py:14
  21.2 1.9 collective-permute-start.1
  23.1 0.0 copy-done.1
  23.1 0.1 slice_reduce_fusion.2
  23.2 0.0 collective-permute-done
  23.2 2.9 %collective-permute-done.1 = bf16[1,1536]{1,0:T(2,128)(2,1)S(1)} collective-permute-done((bf16[1,1536]{1,0:T(2,128)(2,1)S(1)}, bf16[1,1536]{1,0:T(2,128)(2,1)S(1)}, u32[]{:S(2)}, u32[]{:S(2)}) %collective-permute-start.1) | collective-permute-done | bytes 3104 | tf_op jit(solution)/shard_map/ppermute | solution.py:16
  26.1 0.0 copy-start
  26.1 0.0 copy-start.3
  26.1 1.5 convolution_convert_fusion
  27.7 8.3 %collective-permute-start.2 = (bf16[512,1536]{1,0:T(8,128)(2,1)S(1)}, bf16[512,1536]{1,0:T(8,128)(2,1)S(1)}, u32[]{:S(2)}, u32[]{:S(2)}) collective-permute-start(bf16[512,1536]{1,0:T(8,128)(2,1)S(1)} %convolution_convert_fusion), channel_id=1, source_target_pairs={{0,252},{1,253},{2,254},{3,255},{4,248},{5,249},{6,250},{7,251},{8... | collective-permute-start | bytes 4718600 | tf_op jit(solution)/shard_map/ppermute | solution.py:38
  35.9 0.0 copy-done
  36.0 0.0 copy-start.2
  36.0 39.6 %collective-permute-done.2 = bf16[512,1536]{1,0:T(8,128)(2,1)S(1)} collective-permute-done((bf16[512,1536]{1,0:T(8,128)(2,1)S(1)}, bf16[512,1536]{1,0:T(8,128)(2,1)S(1)}, u32[]{:S(2)}, u32[]{:S(2)}) %collective-permute-start.2) | collective-permute-done | bytes 1572896 | tf_op jit(solution)/shard_map/ppermute | solution.py:38
  75.6 64.0 %all-gather.3.cloned.1.call-done = bf16[1536,1536]{1,0:T(8,128)(2,1)} async-done(((bf16[48,1536]{1,0:T(8,128)(2,1)}), bf16[1536,1536]{1,0:T(8,128)(2,1)}) %all-gather.3.cloned.1.call-update) | async-done | bytes 4718608 | tf_op jit(solution)/shard_map/all_gather | solution.py:44
  139.6 0.0 copy-done.3
  139.6 6.6 %fusion.20 = bf16[512,1536]{1,0:T(8,128)(2,1)} fusion(bf16[512,1536]{1,0:T(8,128)(2,1)S(1)} %collective-permute-done.2, bf16[1536,1536]{1,0:T(8,128)(2,1)} %all-gather.3.cloned.1.call-done, f32[1536]{0:T(1024)S(1)} %copy-done.3), kind=kOutput, calls=%fused_computation.31 | convolution fusion | flops 2423783424 | bytes 7870464 | tf_op jit(solution)/shard_map/dot_general | solution.py:58
  146.2 70.0 %all-gather.5.cloned.1.call-done = bf16[1536,3840]{0,1:T(8,128)(2,1)} async-done(((bf16[1536,120]{0,1:T(8,128)(2,1)}), bf16[1536,3840]{0,1:T(8,128)(2,1)}) %all-gather.5.cloned.1.call-update) | async-done | bytes 11796496 | tf_op jit(solution)/shard_map/all_gather | solution.py:45
  216.2 0.0 copy-done.2
  216.2 15.1 %fusion.1 = bf16[512,3840]{1,0:T(8,128)(2,1)} fusion(bf16[512,1536]{1,0:T(8,128)(2,1)} %fusion.20, bf16[1536,3840]{0,1:T(8,128)(2,1)} %all-gather.5.cloned.1.call-done, f32[3840]{0:T(1024)S(1)} %copy-done.2), kind=kOutput, calls=%fused_computation.4 | convolution fusion | flops 6055526400 | bytes 17316864 | tf_op jit(solution)/shard_map/dot_general | solution.py:60
  231.4 6.3 %copy.9 = bf16[512,3840]{0,1:T(8,128)(2,1)} copy(bf16[512,3840]{1,0:T(8,128)(2,1)} %fusion.1) | data formatting | bytes 7864320 | tf_op jit(solution)/shard_map/convert_element_type | solution.py:61
  237.6 14.5 %gather_fusion = bf16[3840,512]{1,0:T(8,128)(2,1)} fusion(bf16[512,3840]{0,1:T(8,128)(2,1)} %copy.9, s32[4096]{0:T(1024)S(1)} %pad_clamp_fusion), kind=kCustom, calls=%fused_computation | custom fusion | bytes 7879680 | tf_op jit(solution)/shard_map/jit(_take)/gather | solution.py:64
  252.1 6.3 %copy.10 = bf16[3840,512]{0,1:T(8,128)(2,1)} copy(bf16[3840,512]{1,0:T(8,128)(2,1)} %gather_fusion) | data formatting | bytes 7864320 | tf_op jit(solution)/shard_map/jit(_take)/gather | solution.py:64
  258.4 20.7 %fusion.4 = bf16[1,512,3840]{2,1,0:T(8,128)(2,1)} fusion(bf16[1536,3840]{0,1:T(8,128)(2,1)} %all-gather.5.cloned.1.call-done, bf16[3840,512]{0,1:T(8,128)(2,1)} %copy.10, f32[3840]{0:T(1024)S(1)} %copy-done.2, pred[3840]{0:T(1024)(128)(4,1)S(1)} %compare_and_fusion, bf16[1536,1536]{1,0:T(8,128)(2,1)} %all-gather.3.cloned.1.call-done, ...), kind=kOutput, calls=%fused_computation.8 | convolution fusion | flops 8502902784 | bytes 26002176 | tf_op jit(solution)/shard_map/dot_general | solution.py:60
  (4 shorter events, 0.0 us)
Async XLA Ops:
  6.5 133.1 %all-gather.3.cloned.1.call-start = ((), (), s32[]{:S(2)}) async-start(), calls=%async_computation | async-start | bytes 4866048 | tf_op jit(solution)/shard_map/all_gather | solution.py:44
  7.3 209.0 %all-gather.5.cloned.1.call-start = ((), (), s32[]{:S(2)}) async-start(), calls=%async_computation.1 | async-start | bytes 12165120 | tf_op jit(solution)/shard_map/all_gather | solution.py:45
  13.7 9.4 %copy-start.1 = (f32[3,1536]{1,0:T(4,128)S(1)}, f32[3,1536]{1,0:T(4,128)}, u32[]{:S(2)}) copy-start(f32[3,1536]{1,0:T(4,128)} %param.10) | copy-start | bytes 55300
  16.6 6.6 %collective-permute-start = (bf16[1,1536]{1,0:T(2,128)(2,1)S(1)}, bf16[1,1536]{1,0:T(2,128)(2,1)S(1)}, u32[]{:S(2)}, u32[]{:S(2)}) collective-permute-start(bf16[1,1536]{1,0:T(2,128)(2,1)S(1)} %get-tuple-element.8), channel_id=1, source_target_pairs={{0,8},{8,16},{16,24},{24,32},{32,40},{40,48},{48,56},{56,64},{64,7... | collective-permute-start | bytes 9224 | tf_op jit(solution)/shard_map/ppermute | solution.py:14
  21.2 4.9 %collective-permute-start.1 = (bf16[1,1536]{1,0:T(2,128)(2,1)S(1)}, bf16[1,1536]{1,0:T(2,128)(2,1)S(1)}, u32[]{:S(2)}, u32[]{:S(2)}) collective-permute-start(bf16[1,1536]{1,0:T(2,128)(2,1)S(1)} %get-tuple-element.9), channel_id=1, source_target_pairs={{8,0},{16,8},{24,16},{32,24},{40,32},{48,40},{56,48},{64,56},{72,6... | collective-permute-start | bytes 9224 | tf_op jit(solution)/shard_map/ppermute | solution.py:16
  26.1 9.8 %copy-start = (s32[3840]{0:T(1024)S(1)}, s32[3840]{0:T(1024)}, u32[]{:S(2)}) copy-start(s32[3840]{0:T(1024)} %param.15) | copy-start | bytes 46084
  26.1 113.5 %copy-start.3 = (f32[1536]{0:T(1024)S(1)}, f32[1536]{0:T(1024)}, u32[]{:S(2)}) copy-start(f32[1536]{0:T(1024)} %param.12) | copy-start | bytes 18436
  27.7 48.0 %collective-permute-start.2 = (bf16[512,1536]{1,0:T(8,128)(2,1)S(1)}, bf16[512,1536]{1,0:T(8,128)(2,1)S(1)}, u32[]{:S(2)}, u32[]{:S(2)}) collective-permute-start(bf16[512,1536]{1,0:T(8,128)(2,1)S(1)} %convolution_convert_fusion), channel_id=1, source_target_pairs={{0,252},{1,253},{2,254},{3,255},{4,248},{5,249},{6,250},{7,251},{8... | collective-permute-start | bytes 4718600 | tf_op jit(solution)/shard_map/ppermute | solution.py:38
  36.0 180.3 %copy-start.2 = (f32[3840]{0:T(1024)S(1)}, f32[3840]{0:T(1024)}, u32[]{:S(2)}) copy-start(f32[3840]{0:T(1024)} %param.14) | copy-start | bytes 46084
Sparse Core Ops, SparseCore 0:
  9.2 130.4 all-gather.2
  141.5 74.6 all-gather.4

commit v2 on v1

v2 whole, which is shorter than its diff:
```python
import jax
import jax.numpy as jnp
from jax import lax
from jax.experimental import pallas as pl
from jax.experimental.pallas import tpu as pltpu
from jax.sharding import PartitionSpec as P

ROWS = 512
D = 1536
TRACKS = 3840
SHARD = 120
LANES = 128
BLOCKS = 16
SEP_ROWS = 48
QUARTER = 384
CHUNKS = 4
CHUNK = ROWS // CHUNKS
DYS = (1, 3, 2)


def with_halo(cells, axis, width):
    count = lax.axis_size(axis)
    ends = count - 1
    head = lax.slice_in_dim(cells, 0, width, axis=0)
    tail = lax.slice_in_dim(cells, cells.shape[0] - width, cells.shape[0], axis=0)
    return jnp.concatenate(
        [
            lax.ppermute(tail, axis, [(i, (i + 1) % count) for i in range(ends)]),
            cells,
            lax.ppermute(head, axis, [((i + 1) % count, i) for i in range(ends)]),
        ],
        axis=0,
    )


def reversed_rows(x):
    rows = x.shape[0]
    r = lax.broadcasted_iota(jnp.int32, (rows, rows), 0)
    c = lax.broadcasted_iota(jnp.int32, (rows, rows), 1)
    flip = (r + c == rows - 1).astype(x.dtype)
    return jnp.dot(flip, x, preferred_element_type=jnp.float32).astype(x.dtype)


def gelu(v):
    return 0.5 * v * (1.0 + jnp.tanh(0.7978845608028654 * (v + 0.044715 * v * v * v)))


def softplus(v):
    return jnp.maximum(v, 0.0) + jnp.log1p(jnp.exp(-jnp.abs(v)))


def kernel(
    dw, rev, sep_in, head_in, sep_b, head_b, pos,
    out,
    wsep, whead, mirrored, feat, hown, hpart, stage,
    local_sem, ex_send, ex_recv, z_send, z_recv, y_send, y_recv, x_send, x_recv,
    s_send, s_recv, out_sem,
):
    s = lax.axis_index("seq")
    b = lax.axis_index("batch")
    c = s % 2
    y = (s // 2) % 4
    zl = s // 8
    x = b // 2
    zh = b % 2
    z = zh * 4 + zl
    u = (5 - zl) % 4

    def device(zz, yy, xx, cc):
        return {"seq": ((zz % 4) * 4 + yy) * 2 + cc, "batch": xx * 2 + zz // 4}

    mirror = {"seq": 31 - s, "batch": (b + 4) % 8}
    sibling = device(z, y, x, 1 - c)
    z_dev = [None] + [device((z + u - (u + k) % 4 + 8) % 8, y, x, c) for k in (1, 2, 3)]
    y_dev = {d: device(z, (y + d) % 4, x, c) for d in (1, 2, 3)}
    x_dev = {d: device(z, y, (x + d) % 4, c) for d in (1, 2, 3)}

    barrier = pltpu.get_barrier_semaphore()
    peers = [mirror, sibling] + z_dev[1:] + list(y_dev.values()) + list(x_dev.values())
    for peer in peers:
        pl.semaphore_signal(barrier, inc=1, device_id=peer, device_id_type=pl.DeviceIdType.MESH)
    pl.semaphore_wait(barrier, len(peers))

    def slot(k, dy):
        return ((zl + k) % 4) * 4 + (y + dy) % 4

    def view(p, j, cc, q=None):
        if p == 0:
            rows = pl.ds(pl.multiple_of((j * 2 + cc) * SEP_ROWS, 16), SEP_ROWS)
            if q is None:
                return wsep.at[rows, :]
            return wsep.at[rows, pl.ds(pl.multiple_of(q * QUARTER, LANES), QUARTER)]
        lanes = pl.ds(pl.multiple_of(cc * LANES, LANES), LANES)
        if q is None:
            return whead.at[j, :, lanes]
        return whead.at[j, pl.ds(pl.multiple_of(q * QUARTER, LANES), QUARTER), lanes]

    def own_view(p, q=None):
        if p == 0:
            if q is None:
                return sep_in
            return sep_in.at[:, pl.ds(pl.multiple_of(q * QUARTER, LANES), QUARTER)]
        if q is None:
            return head_in
        return head_in.at[pl.ds(pl.multiple_of(q * QUARTER, LANES), QUARTER), :]

    def copy(src, dst, send, recv, to):
        return pltpu.make_async_remote_copy(
            src_ref=src, dst_ref=dst, send_sem=send, recv_sem=recv,
            device_id=to, device_id_type=pl.DeviceIdType.MESH,
        )

    def z_copy(p, k):
        return copy(own_view(p), view(p, slot(0, 0), c), z_send.at[p, k - 1], z_recv.at[p, k - 1], z_dev[k])

    def y_copy(p, k, d):
        i = DYS.index(d)
        q = x if d == 2 else None
        src = own_view(p, q) if k == 0 else view(p, slot(k, 0), c, q)
        return copy(src, view(p, slot(k, 0), c, q), y_send.at[p, k, i], y_recv.at[p, k, i], y_dev[d])

    def x_copy(p, k, d):
        ref = view(p, slot(k, 2), c, x)
        return copy(ref, ref, x_send.at[p, k, d - 1], x_recv.at[p, k, d - 1], x_dev[d])

    def s_copy(p, k, dy):
        src = own_view(p) if k == 0 and dy == 0 else view(p, slot(k, dy), c)
        return copy(src, view(p, slot(k, dy), c), s_send.at[p, k, dy], s_recv.at[p, k, dy], sibling)

    def arrived(dst, recv):
        copy(dst, dst, s_send.at[0, 0, 0], recv, sibling).wait_recv()

    def z_wait(p, k):
        arrived(view(p, slot(k, 0), c), z_recv.at[p, k - 1])

    def y_wait(p, k, d):
        i = DYS.index((4 - d) % 4)
        q = x if d == 2 else None
        arrived(view(p, slot(k, d), c, q), y_recv.at[p, k, i])

    def x_wait(p, k, d):
        arrived(view(p, slot(k, 2), c, (x + 4 - d) % 4), x_recv.at[p, k, d - 1])

    def s_wait(p, k, dy):
        arrived(view(p, slot(k, dy), 1 - c), s_recv.at[p, k, dy])

    def ex_copy(i):
        rows = pl.ds(i * CHUNK, CHUNK)
        return copy(rev.at[rows, :], mirrored.at[rows, :], ex_send.at[i], ex_recv.at[i], mirror)

    def spread(p, k):
        for d in (2, 1, 3):
            y_copy(p, k, d).start()
        s_copy(p, k, 0).start()

    locals_ = [
        pltpu.make_async_copy(own_view(p), view(p, slot(0, 0), c), local_sem.at[p]) for p in (0, 1)
    ]
    for cp in locals_:
        cp.start()
    for p in (0, 1):
        for k in (1, 2, 3):
            z_copy(p, k).start()
        spread(p, 0)
        if p == 0:
            for i in range(CHUNKS):
                ex_copy(i).start()

    def z_stage(p):
        for k in (1, 2, 3):
            z_wait(p, k)
            spread(p, k)

    def q_stage(p):
        for k in range(4):
            y_wait(p, k, 2)
            for d in (2, 1, 3):
                x_copy(p, k, d).start()

    def last_stage(p):
        for k in range(4):
            for d in (1, 3):
                y_wait(p, k, d)
                s_copy(p, k, d).start()
        for k in range(4):
            for d in (1, 3, 2):
                x_wait(p, k, d)
            s_copy(p, k, 2).start()

    def from_sibling(p):
        for k in range(4):
            for dy in range(4):
                s_wait(p, k, dy)

    z_stage(0)
    q_stage(0)
    z_stage(1)
    last_stage(0)
    for cp in locals_:
        cp.wait()
    from_sibling(0)

    def features(block):
        @pl.loop(0, D // 256)
        def _(n):
            cols = pl.ds(pl.multiple_of(n * 256, 256), 256)
            v = jnp.dot(block[...], wsep[:, cols], preferred_element_type=jnp.float32)
            feat[:, cols] = gelu(v + sep_b[:, cols]).astype(jnp.bfloat16)

    def head(dst):
        @pl.loop(0, BLOCKS)
        def _(j):
            cols = pl.ds(pl.multiple_of(j * 256, 256), 256)
            v = jnp.dot(feat[...], whead[j], preferred_element_type=jnp.float32)
            dst[:, cols] = softplus(v + head_b[:, cols]).astype(jnp.bfloat16)

    features(dw)
    q_stage(1)
    last_stage(1)
    from_sibling(1)
    head(hown)
    for i in range(CHUNKS):
        rows = pl.ds(i * CHUNK, CHUNK)
        arrived(mirrored.at[rows, :], ex_recv.at[i])
    features(mirrored)
    head(hpart)

    def out_copy(n, i):
        cols = pl.ds(pl.multiple_of(n * 256, 256), 256)
        return pltpu.make_async_copy(stage.at[i], out.at[:, cols], out_sem.at[i])

    row = lax.broadcasted_iota(jnp.int32, (512, 256), 0)
    col = lax.broadcasted_iota(jnp.int32, (1, 256), 1)
    tiles = TRACKS // 256

    def ones_at(place):
        return jnp.where(row == place, 1.0, 0.0).astype(jnp.bfloat16)

    @pl.loop(0, tiles)
    def _(n):
        i = n % 2
        cols = pl.ds(pl.multiple_of(n * 256, 256), 256)
        track = n * 256 + col
        place = (track // SHARD) * LANES + track % SHARD - n * 256
        near = hown[:, pl.ds(pl.multiple_of(n * 256, 256), 512)]
        total = jnp.dot(near, ones_at(place), preferred_element_type=jnp.float32)
        source = pos[:, cols]
        for m in range(BLOCKS // 2):
            total += jnp.dot(
                hpart[:, m * 512:(m + 1) * 512],
                ones_at(source - m * 512),
                preferred_element_type=jnp.float32,
            )

        @pl.when(n >= 2)
        def _():
            out_copy(n - 2, i).wait()

        stage[i] = (0.5 * total).astype(jnp.bfloat16)
        out_copy(n, i).start()

    for n in (tiles - 2, tiles - 1):
        out_copy(n, n % 2).wait()

    for i in range(CHUNKS):
        ex_copy(i).wait_send()
    for p in (0, 1):
        for k in range(4):
            if k:
                z_copy(p, k).wait_send()
            for d in (1, 2, 3):
                y_copy(p, k, d).wait_send()
                x_copy(p, k, d).wait_send()
            for dy in range(4):
                s_copy(p, k, dy).wait_send()


def fused(dw, rev, sep_in, head_in, sep_b, head_b, pos):
    dma = pltpu.SemaphoreType.DMA
    vmem = pl.BlockSpec(memory_space=pltpu.VMEM)
    return pl.pallas_call(
        kernel,
        out_shape=jax.ShapeDtypeStruct((ROWS, TRACKS), jnp.bfloat16),
        in_specs=[vmem] * 7,
        out_specs=pl.BlockSpec(memory_space=pl.ANY),
        scratch_shapes=[
            pltpu.VMEM((D, D), jnp.bfloat16),
            pltpu.VMEM((BLOCKS, D, 256), jnp.bfloat16),
            pltpu.VMEM((ROWS, D), jnp.bfloat16),
            pltpu.VMEM((ROWS, D), jnp.bfloat16),
            pltpu.VMEM((ROWS, BLOCKS * 256), jnp.bfloat16),
            pltpu.VMEM((ROWS, BLOCKS * 256), jnp.bfloat16),
            pltpu.VMEM((2, ROWS, 256), jnp.bfloat16),
            dma((2,)),
            dma((CHUNKS,)),
            dma((CHUNKS,)),
            dma((2, 3)),
            dma((2, 3)),
            dma((2, 4, 3)),
            dma((2, 4, 3)),
            dma((2, 4, 3)),
            dma((2, 4, 3)),
            dma((2, 4, 4)),
            dma((2, 4, 4)),
            dma((2,)),
        ],
        compiler_params=pltpu.CompilerParams(
            collective_id=0, has_side_effects=True, vmem_limit_bytes=60 * 1024 * 1024
        ),
    )(dw, rev, sep_in, head_in, sep_b, head_b, pos)


def per_device(
    coarse, skip, depth_kernel, sep_weight, sep_bias, head_weight, head_bias, strand_pair
):
    upsampled = jnp.repeat(coarse[0].astype(jnp.float32), 2, axis=0)
    merged = (upsampled + skip[0]).astype(jnp.bfloat16)
    padded = with_halo(merged, "seq", 1)
    depthwise = (
        depth_kernel[0] * padded[:-2]
        + depth_kernel[1] * padded[1:-1]
        + depth_kernel[2] * padded[2:]
    )
    depthwise = depthwise.astype(jnp.bfloat16)
    pos = (strand_pair // SHARD) * LANES + strand_pair % SHARD
    bias = jnp.pad(head_bias.reshape(-1, SHARD), ((0, 0), (0, LANES - SHARD)))
    preds = fused(
        depthwise,
        reversed_rows(depthwise),
        sep_weight,
        jnp.pad(head_weight, ((0, 0), (0, LANES - SHARD))),
        sep_bias[None],
        bias.reshape(1, -1),
        pos[None],
    )
    return preds[None]


def solution(mesh):
    in_specs = (
        P("batch", "seq", None),
        P("batch", "seq", None),
        P(),
        P("seq", None),
        P(),
        P(None, "seq"),
        P(),
        P(),
    )
    return jax.shard_map(
        per_device,
        mesh=mesh,
        in_specs=in_specs,
        out_specs=P("batch", "seq", None),
        check_vma=False,
    )
```

time: 286 us -> 198 us (0.69)
  the two profiles are of different devices: /device:TPU:1 before, /device:TPU:87 now
where the time goes in v2:
time: 198 us
  Pallas kernels  173 us (87%)
  local copies, waits for them, and re-layouts  11.8 us (6%)
  starting transfers between devices  5.39 us (3%)
  other arithmetic  5.28 us (3%)
  matrix products  2.14 us (1%)
    pallas_call x1, Pallas kernels, fused(): pl.pallas_call(kernel, out_shape=jax.ShapeDtypeStruct((ROWS, TRACKS), jnp...  173 us
    unnamed x14, local copies, waits for them, and re-layouts  4.54 us
  transfers between devices with their start and end apart: 2, of which 0 were waited for; matrix products, arithmetic and copies ran while one was open for 2% of the time, Pallas kernels for 0%

profile of v2, /device:TPU:87, one launch (start us, length us, event | category | flops | bytes accessed | tf_op | source)
XLA Modules:
  0.0 197.6 jit_solution(10399676034735286306)
XLA Ops:
  0.0 1.3 bitcast_convert_fusion
  1.3 1.1 broadcast_in_dim.12
  2.4 3.3 %reshape.13 = f32[512,1536]{1,0:T(8,128)} reshape(f32[256,2,1536]{2,1,0:T(2,128)S(1)} %broadcast_in_dim.12) | data formatting | bytes 6291456 | tf_op jit(solution)/shard_map/reshape | solution.py:316
  5.7 0.0 copy-start.2
  5.7 0.0 copy-start.4
  5.7 0.0 copy-start.5
  5.7 0.0 copy-start.3
  5.7 0.0 copy-start.1
  5.8 2.9 %fusion = bf16[512,1536]{1,0:T(8,128)(2,1)S(1)} fusion(f32[512,1536]{1,0:T(8,128)} %reshape.13, bf16[1,512,1536]{2,1,0:T(8,128)(2,1)} %param.9), kind=kLoop, calls=%fused_computation.1 | loop fusion | flops 2359296 | bytes 6291456 | tf_op jit(solution)/shard_map/convert_element_type | solution.py:317
  8.7 3.5 %collective-permute-start = (bf16[1,1536]{1,0:T(2,128)(2,1)S(1)}, bf16[1,1536]{1,0:T(2,128)(2,1)S(1)}, u32[]{:S(2)}, u32[]{:S(2)}) collective-permute-start(bf16[1,1536]{1,0:T(2,128)(2,1)S(1)} %get-tuple-element.8), channel_id=1, source_target_pairs={{0,8},{8,16},{16,24},{24,32},{32,40},{40,48},{48,56},{56,64},{64,7... | collective-permute-start | bytes 9224 | tf_op jit(solution)/shard_map/ppermute | solution.py:28
  12.1 1.9 collective-permute-start.1
  14.1 0.0 copy-done.2
  14.1 0.0 copy-done.4
  14.1 0.1 slice_reduce_fusion.2
  14.2 0.0 copy-done.5
  14.2 0.6 broadcast_in_dim.13.sep_b
  14.8 0.0 copy-done.3
  14.8 0.1 reshape.14
  14.9 0.6 broadcast_in_dim.14.pos
  15.5 0.0 copy-done.1
  15.5 0.2 copy.9
  15.7 0.6 pad.9
  16.3 0.9 pad.8.head_in
  17.2 0.0 collective-permute-done
  17.2 0.0 collective-permute-done.1
  17.2 1.1 add_convert_fusion.dw
  18.3 0.0 copy-start
  18.3 2.1 %convolution_convert_fusion.rev = bf16[512,1536]{1,0:T(8,128)(2,1)} fusion(bf16[512,1536]{1,0:T(8,128)(2,1)S(1)} %add_convert_fusion.dw), kind=kOutput, calls=%fused_computation.3 | convolution fusion | flops 806617088 | bytes 3145728 | tf_op jit(solution)/shard_map/dot_general | solution.py:41
  20.4 0.0 copy-done
  20.4 172.8 %shard_map.82 = bf16[512,3840]{1,0:T(8,128)(2,1)} custom-call(bf16[512,1536]{1,0:T(8,128)(2,1)} %copy-done, bf16[512,1536]{1,0:T(8,128)(2,1)} %convolution_convert_fusion.rev, bf16[48,1536]{1,0:T(8,128)(2,1)} %sep_in.1, bf16[1536,128]{1,0:T(8,128)(2,1)} %pad.8.head_in, f32[1,1536]{1,0:T(1,128)} %broadcast_in_dim.13.sep_b, f32[1,4096]{1,0:T(1,128)} %bitcast.10, ...), custom_call_target="tpu_custom_call" | custom-call | tf_op jit(solution)/shard_map/pallas_call | solution.py:281
  193.3 4.3 %copy.11 = bf16[1,512,3840]{2,1,0:T(8,128)(2,1)} copy(bf16[1,512,3840]{2,1,0:T(8,128)(2,1)} %bitcast.9) | data formatting | bytes 7864320
  (2 shorter events, 0.0 us)
Async XLA Ops:
  5.7 8.3 %copy-start.2 = (s32[3840]{0:T(1024)S(1)}, s32[3840]{0:T(1024)}, u32[]{:S(2)}) copy-start(s32[3840]{0:T(1024)} %param.15) | copy-start | bytes 46084
  5.7 8.4 %copy-start.4 = (f32[3,1536]{1,0:T(4,128)S(1)}, f32[3,1536]{1,0:T(4,128)}, u32[]{:S(2)}) copy-start(f32[3,1536]{1,0:T(4,128)} %param.10) | copy-start | bytes 55300
  5.7 8.4 %copy-start.5 = (f32[1536]{0:T(1024)S(1)}, f32[1536]{0:T(1024)}, u32[]{:S(2)}) copy-start(f32[1536]{0:T(1024)} %param.12) | copy-start | bytes 18436
  5.7 9.0 %copy-start.3 = (f32[3840]{0:T(1024)S(1)}, f32[3840]{0:T(1024)}, u32[]{:S(2)}) copy-start(f32[3840]{0:T(1024)} %param.14) | copy-start | bytes 46084
  5.7 9.7 %copy-start.1 = (bf16[1536,120]{0,1:T(8,128)(2,1)S(1)}, bf16[1536,120]{0,1:T(8,128)(2,1)}, u32[]{:S(2)}) copy-start(bf16[1536,120]{0,1:T(8,128)(2,1)} %param.13) | copy-start | bytes 1105924
  8.7 8.5 %collective-permute-start = (bf16[1,1536]{1,0:T(2,128)(2,1)S(1)}, bf16[1,1536]{1,0:T(2,128)(2,1)S(1)}, u32[]{:S(2)}, u32[]{:S(2)}) collective-permute-start(bf16[1,1536]{1,0:T(2,128)(2,1)S(1)} %get-tuple-element.8), channel_id=1, source_target_pairs={{0,8},{8,16},{16,24},{24,32},{32,40},{40,48},{48,56},{56,64},{64,7... | collective-permute-start | bytes 9224 | tf_op jit(solution)/shard_map/ppermute | solution.py:28
  12.1 5.1 %collective-permute-start.1 = (bf16[1,1536]{1,0:T(2,128)(2,1)S(1)}, bf16[1,1536]{1,0:T(2,128)(2,1)S(1)}, u32[]{:S(2)}, u32[]{:S(2)}) collective-permute-start(bf16[1,1536]{1,0:T(2,128)(2,1)S(1)} %get-tuple-element.9), channel_id=1, source_target_pairs={{8,0},{16,8},{24,16},{32,24},{40,32},{48,40},{56,48},{64,56},{72,6... | collective-permute-start | bytes 9224 | tf_op jit(solution)/shard_map/ppermute | solution.py:30
  18.3 2.2 %copy-start = (bf16[512,1536]{1,0:T(8,128)(2,1)}, bf16[512,1536]{1,0:T(8,128)(2,1)S(1)}, u32[]{:S(2)}) copy-start(bf16[512,1536]{1,0:T(8,128)(2,1)S(1)} %add_convert_fusion.dw) | copy-start | bytes 4718596

commit v3 on v2

v3 whole, which is shorter than its diff:
```python
import jax
import jax.numpy as jnp
from jax import lax
from jax.experimental import pallas as pl
from jax.experimental.pallas import tpu as pltpu
from jax.sharding import PartitionSpec as P

ROWS = 512
D = 1536
TRACKS = 3840
SHARD = 120
LANES = 128
BLOCKS = 16
SEP_ROWS = 48
QUARTER = 384
CHUNKS = 4
CHUNK = ROWS // CHUNKS
HALF = ROWS // 2
ALL = pl.ds(0, ROWS)
SHARED = (0,)
ORDER = (0, 1, 3, 2)


def gelu(v):
    return 0.5 * v * (1.0 + jnp.tanh(0.7978845608028654 * (v + 0.044715 * v * v * v)))


def softplus(v):
    return jnp.maximum(v, 0.0) + jnp.log1p(jnp.exp(-jnp.abs(v)))


def split(p, e, k):
    return p == 1 and (e == 2 or (e == 3 and k in SHARED))


def kernel(
    coarse, skip, depth, sep_in, head_in, sep_b, head_b, pos,
    out,
    wsep, whead, merged, dw, rev, mirrored, feat, featm, hown, hpart, perm, stage,
    local_sem, halo_send, halo_recv, ex_send, ex_recv, z_send, z_recv, y_send, y_recv,
    x_send, x_recv, s_send, s_recv, out_sem,
):
    s = lax.axis_index("seq")
    b = lax.axis_index("batch")
    c = s % 2
    y = (s // 2) % 4
    zl = s // 8
    x = b // 2
    zh = b % 2
    z = zh * 4 + zl
    u = (5 - zl) % 4
    ys = (y, y + 1 - 2 * (y % 2), (y + 2) % 4, 3 - y)

    def device(zz, yy, xx, cc):
        return {"seq": ((zz % 4) * 4 + yy) * 2 + cc, "batch": xx * 2 + zz // 4}

    mirror = {"seq": 31 - s, "batch": (b + 4) % 8}
    sibling = device(z, y, x, 1 - c)
    left = {"seq": (s + 31) % 32, "batch": b}
    right = {"seq": (s + 1) % 32, "batch": b}
    z_dev = [None] + [device((z + d) % 8, y, x, c) for d in (7, jnp.where(zl < 2, 6, 2), 1)]
    y_dev = [None] + [device(z, ys[e], x, c) for e in (1, 2, 3)]
    x_dev = [None] + [device(z, y, (x + d) % 4, c) for d in (1, 2, 3)]

    barrier = pltpu.get_barrier_semaphore()
    peers = [mirror, left, right] + z_dev[1:] + y_dev[1:] + x_dev[1:]
    for peer in peers:
        pl.semaphore_signal(barrier, inc=1, device_id=peer, device_id_type=pl.DeviceIdType.MESH)
    pl.semaphore_wait(barrier, len(peers))

    def slot(k, e):
        return ((zl + k) % 4) * 4 + ys[e]

    def view(p, j, cc, q=None):
        if p == 0:
            rows = pl.ds(pl.multiple_of((j * 2 + cc) * SEP_ROWS, 16), SEP_ROWS)
            if q is None:
                return wsep.at[rows, :]
            return wsep.at[rows, pl.ds(pl.multiple_of(q * QUARTER, LANES), QUARTER)]
        lanes = pl.ds(pl.multiple_of(cc * LANES, LANES), LANES)
        if q is None:
            return whead.at[j, :, lanes]
        return whead.at[j, pl.ds(pl.multiple_of(q * QUARTER, LANES), QUARTER), lanes]

    def own_view(p, q=None):
        if p == 0:
            if q is None:
                return sep_in
            return sep_in.at[:, pl.ds(pl.multiple_of(q * QUARTER, LANES), QUARTER)]
        if q is None:
            return head_in
        return head_in.at[pl.ds(pl.multiple_of(q * QUARTER, LANES), QUARTER), :]

    def copy(src, dst, send, recv, to):
        return pltpu.make_async_remote_copy(
            src_ref=src, dst_ref=dst, send_sem=send, recv_sem=recv,
            device_id=to, device_id_type=pl.DeviceIdType.MESH,
        )

    def z_copy(p, k):
        return copy(own_view(p), view(p, slot(0, 0), c), z_send.at[p, k - 1], z_recv.at[p, k - 1], z_dev[k])

    def y_copy(p, k, e):
        q = x if split(p, e, k) else None
        src = own_view(p, q) if k == 0 else view(p, slot(k, 0), c, q)
        return copy(src, view(p, slot(k, 0), c, q), y_send.at[p, k, e - 1], y_recv.at[p, k, e - 1], y_dev[e])

    def x_copy(p, k, e, d):
        ref = view(p, slot(k, e), c, x)
        return copy(ref, ref, x_send.at[p, e - 2, k, d - 1], x_recv.at[p, e - 2, k, d - 1], x_dev[d])

    def s_copy(p, k, e):
        src = own_view(p) if k == 0 and e == 0 else view(p, slot(k, e), c)
        return copy(src, view(p, slot(k, e), c), s_send.at[p, k, e], s_recv.at[p, k, e], sibling)

    def arrived(dst, recv):
        copy(dst, dst, s_send.at[0, 0, 0], recv, sibling).wait_recv()

    def z_wait(p, k):
        arrived(view(p, slot(k, 0), c), z_recv.at[p, k - 1])

    def y_wait(p, k, e):
        q = x if split(p, e, k) else None
        arrived(view(p, slot(k, e), c, q), y_recv.at[p, k, e - 1])

    def x_wait(p, k, e, d):
        arrived(view(p, slot(k, e), c, (x + 4 - d) % 4), x_recv.at[p, e - 2, k, d - 1])

    def s_wait(p, k, e):
        arrived(view(p, slot(k, e), 1 - c), s_recv.at[p, k, e])

    def ex_copy(i):
        rows = pl.ds(i * CHUNK, CHUNK)
        return copy(rev.at[rows, :], mirrored.at[rows, :], ex_send.at[i], ex_recv.at[i], mirror)

    middle = (zl == 1) | (zl == 2)

    def ex_some(near, chunks):
        @pl.when(middle if near else jnp.logical_not(middle))
        def _():
            for i in chunks:
                ex_copy(i).start()

    def spread(p, k, es=(2, 3, 1)):
        for e in es:
            y_copy(p, k, e).start()
        if 1 in es:
            s_copy(p, k, 0).start()

    def z_stage(p):
        for k in (1, 3, 2):
            z_wait(p, k)
            spread(p, k)

    def x_stage(p, e, items=ORDER):
        for k in items:
            if split(p, e, k):
                y_wait(p, k, e)
                for d in (2, 1, 3):
                    x_copy(p, k, e, d).start()

    def last_stage(p, e):
        for k in ORDER:
            if split(p, e, k):
                for d in (1, 3, 2):
                    x_wait(p, k, e, d)
            else:
                y_wait(p, k, e)
            s_copy(p, k, e).start()

    def from_sibling(p, e):
        for k in range(4):
            s_wait(p, k, e)

    def tile(n):
        return pl.ds(pl.multiple_of(n * 256, 256), 256)

    def features(block, dst):
        @pl.loop(0, D // 256)
        def _(n):
            v = jnp.dot(block[...], wsep[:, tile(n)], preferred_element_type=jnp.float32)
            dst[:, tile(n)] = gelu(v + sep_b[:, tile(n)]).astype(jnp.bfloat16)

    def head(block, dst, rows, e):
        @pl.loop(0, 4)
        def _(k):
            j = slot(k, e)
            v = jnp.dot(block[...], whead[j], preferred_element_type=jnp.float32)
            dst[rows, tile(j)] = softplus(v + head_b[:, tile(j)]).astype(jnp.bfloat16)

    locals_ = [
        pltpu.make_async_copy(own_view(p), view(p, slot(0, 0), c), local_sem.at[p]) for p in (0, 1)
    ]
    for cp in locals_:
        cp.start()
    for p in (0, 1):
        for k in (1, 3, 2):
            z_copy(p, k).start()
        spread(p, 0, (2, 3) if p else (2, 3, 1))

    i0 = lax.broadcasted_iota(jnp.int32, (ROWS, ROWS), 0)
    i1 = lax.broadcasted_iota(jnp.int32, (ROWS, ROWS), 1)
    up = jnp.where(i0[:, :ROWS // 2] // 2 == i1[:, :ROWS // 2], 1.0, 0.0).astype(jnp.bfloat16)

    @pl.loop(0, D // 256)
    def _(n):
        doubled = jnp.dot(up, coarse[:, tile(n)], preferred_element_type=jnp.float32)
        both = (doubled + skip[:, tile(n)].astype(jnp.float32)).astype(jnp.bfloat16)
        merged[8:8 + ROWS, tile(n)] = both.astype(jnp.float32)

    halos = [
        copy(merged.at[pl.ds(8, 8), :], merged.at[pl.ds(8 + ROWS, 8), :], halo_send.at[0], halo_recv.at[0], left),
        copy(merged.at[pl.ds(ROWS, 8), :], merged.at[pl.ds(0, 8), :], halo_send.at[1], halo_recv.at[1], right),
    ]
    for cp in halos:
        cp.start()
    flip = jnp.where(i0 + i1 == ROWS - 1, 1.0, 0.0).astype(jnp.bfloat16)
    for cp in halos:
        cp.wait_recv()

    @pl.when(s == 0)
    def _():
        merged[0:8, :] = jnp.zeros((8, D), jnp.float32)

    @pl.when(s == 31)
    def _():
        merged[8 + ROWS:16 + ROWS, :] = jnp.zeros((8, D), jnp.float32)

    @pl.loop(0, D // 256)
    def _(n):
        taps = depth[:, tile(n)]
        v = (
            taps[0:1] * merged[7:7 + ROWS, tile(n)]
            + taps[1:2] * merged[8:8 + ROWS, tile(n)]
            + taps[2:3] * merged[9:9 + ROWS, tile(n)]
        ).astype(jnp.bfloat16)
        dw[:, tile(n)] = v
        rev[:, tile(n)] = jnp.dot(flip, v, preferred_element_type=jnp.float32).astype(jnp.bfloat16)

    row = lax.broadcasted_iota(jnp.int32, (512, 256), 0)
    col = lax.broadcasted_iota(jnp.int32, (1, 256), 1)
    tiles = TRACKS // 256

    def ones_at(place, rows):
        return jnp.where(row[:rows] == place, 1.0, 0.0).astype(jnp.bfloat16)

    def moved(rows, n, es):
        source = pos[:, tile(n)]
        total = 0.0
        for e in es:
            for k in range(4):
                j = slot(k, e)
                total += jnp.dot(
                    hpart[rows, tile(j)],
                    ones_at(source - j * 256, 256),
                    preferred_element_type=jnp.float32,
                )
        return total

    def half_arrives(h):
        for i in range(h * CHUNKS // 2, (h + 1) * CHUNKS // 2):
            arrived(mirrored.at[pl.ds(i * CHUNK, CHUNK), :], ex_recv.at[i])
        rows = pl.ds(h * HALF, HALF)
        features(mirrored.at[rows, :], featm.at[rows, :])

    def partner(h, e):
        rows = pl.ds(h * HALF, HALF)
        head(featm.at[rows, :], hpart, rows, e)

    def early(h):
        rows = pl.ds(h * HALF, HALF)

        @pl.loop(0, tiles)
        def _(n):
            perm[rows, tile(n)] = moved(rows, n, (0, 1, 2)).astype(jnp.bfloat16)

    ex_some(True, (0, 1, 2, 3))
    z_stage(0)
    y_copy(1, 0, 1).start()
    s_copy(1, 0, 0).start()
    x_stage(0, 2)
    ex_some(False, (0, 1))
    z_stage(1)
    x_stage(1, 3)
    x_stage(1, 2, (0,))
    ex_some(False, (2,))
    for e in (1, 3, 2):
        last_stage(0, e)
    for cp in locals_:
        cp.wait()
    for e in (0, 1, 3, 2):
        from_sibling(0, e)
    x_stage(1, 2, (1,))
    ex_some(False, (3,))
    features(dw, feat)
    x_stage(1, 2, (3,))
    from_sibling(1, 0)
    head(feat, hown, ALL, 0)
    x_stage(1, 2, (2,))
    half_arrives(0)
    partner(0, 0)
    last_stage(1, 1)
    from_sibling(1, 1)
    head(feat, hown, ALL, 1)
    partner(0, 1)
    last_stage(1, 2)
    from_sibling(1, 2)
    head(feat, hown, ALL, 2)
    partner(0, 2)
    early(0)
    half_arrives(1)
    for e in (0, 1, 2):
        partner(1, e)
    last_stage(1, 3)
    early(1)
    from_sibling(1, 3)
    head(feat, hown, ALL, 3)
    head(featm, hpart, ALL, 3)

    def out_copy(n, i):
        return pltpu.make_async_copy(stage.at[i], out.at[:, tile(n)], out_sem.at[i])

    @pl.loop(0, tiles)
    def _(n):
        i = n % 2
        track = n * 256 + col
        place = (track // SHARD) * LANES + track % SHARD - n * 256
        near = hown[:, pl.ds(pl.multiple_of(n * 256, 256), 512)]
        total = jnp.dot(near, ones_at(place, 512), preferred_element_type=jnp.float32)
        total += moved(ALL, n, (3,))
        total += perm[:, tile(n)].astype(jnp.float32)

        @pl.when(n >= 2)
        def _():
            out_copy(n - 2, i).wait()

        stage[i] = (0.5 * total).astype(jnp.bfloat16)
        out_copy(n, i).start()

    for n in (tiles - 2, tiles - 1):
        out_copy(n, n % 2).wait()

    for cp in halos:
        cp.wait_send()
    for i in range(CHUNKS):
        ex_copy(i).wait_send()
    for p in (0, 1):
        for k in range(4):
            if k:
                z_copy(p, k).wait_send()
            for e in (1, 2, 3):
                y_copy(p, k, e).wait_send()
                if split(p, e, k):
                    for d in (1, 2, 3):
                        x_copy(p, k, e, d).wait_send()
            for e in range(4):
                s_copy(p, k, e).wait_send()


def fused(coarse, skip, depth, sep_in, head_in, sep_b, head_b, pos):
    dma = pltpu.SemaphoreType.DMA
    vmem = pl.BlockSpec(memory_space=pltpu.VMEM)
    return pl.pallas_call(
        kernel,
        out_shape=jax.ShapeDtypeStruct((ROWS, TRACKS), jnp.bfloat16),
        in_specs=[vmem] * 8,
        out_specs=pl.BlockSpec(memory_space=pl.ANY),
        scratch_shapes=[
            pltpu.VMEM((D, D), jnp.bfloat16),
            pltpu.VMEM((BLOCKS, D, 256), jnp.bfloat16),
            pltpu.VMEM((ROWS + 16, D), jnp.float32),
            pltpu.VMEM((ROWS, D), jnp.bfloat16),
            pltpu.VMEM((ROWS, D), jnp.bfloat16),
            pltpu.VMEM((ROWS, D), jnp.bfloat16),
            pltpu.VMEM((ROWS, D), jnp.bfloat16),
            pltpu.VMEM((ROWS, D), jnp.bfloat16),
            pltpu.VMEM((ROWS, BLOCKS * 256), jnp.bfloat16),
            pltpu.VMEM((ROWS, BLOCKS * 256), jnp.bfloat16),
            pltpu.VMEM((ROWS, TRACKS), jnp.bfloat16),
            pltpu.VMEM((2, ROWS, 256), jnp.bfloat16),
            dma((2,)),
            dma((2,)),
            dma((2,)),
            dma((CHUNKS,)),
            dma((CHUNKS,)),
            dma((2, 3)),
            dma((2, 3)),
            dma((2, 4, 3)),
            dma((2, 4, 3)),
            dma((2, 2, 4, 3)),
            dma((2, 2, 4, 3)),
            dma((2, 4, 4)),
            dma((2, 4, 4)),
            dma((2,)),
        ],
        compiler_params=pltpu.CompilerParams(
            collective_id=0, has_side_effects=True, vmem_limit_bytes=60 * 1024 * 1024
        ),
    )(coarse, skip, depth, sep_in, head_in, sep_b, head_b, pos)


def per_device(
    coarse, skip, depth_kernel, sep_weight, sep_bias, head_weight, head_bias, strand_pair
):
    pos = (strand_pair // SHARD) * LANES + strand_pair % SHARD
    bias = jnp.pad(head_bias.reshape(-1, SHARD), ((0, 0), (0, LANES - SHARD)))
    preds = fused(
        coarse[0],
        skip[0],
        depth_kernel,
        sep_weight,
        jnp.pad(head_weight, ((0, 0), (0, LANES - SHARD))),
        sep_bias[None],
        bias.reshape(1, -1),
        pos[None],
    )
    return preds[None]


def solution(mesh):
    in_specs = (
        P("batch", "seq", None),
        P("batch", "seq", None),
        P(),
        P("seq", None),
        P(),
        P(None, "seq"),
        P(),
        P(),
    )
    return jax.shard_map(
        per_device,
        mesh=mesh,
        in_specs=in_specs,
        out_specs=P("batch", "seq", None),
        check_vma=False,
    )
```

time: 198 us -> 166 us (0.84)
  the two profiles are of different devices: /device:TPU:87 before, /device:TPU:1 now
where the time goes in v3:
time: 166 us
  Pallas kernels  155 us (93%)
  local copies, waits for them, and re-layouts  9.63 us (6%)
    pallas_call x1, Pallas kernels, fused(): pl.pallas_call(kernel, out_shape=jax.ShapeDtypeStruct((ROWS, TRACKS), jnp...  155 us
    unnamed x2, local copies, waits for them, and re-layouts  5.5 us

profile of v3, /device:TPU:1, one launch (start us, length us, event | category | flops | bytes accessed | tf_op | source)
XLA Modules:
  0.0 165.6 jit_solution(9839288898840115672)
XLA Ops:
  0.0 1.3 broadcast_in_dim.9.sep_b
  1.3 0.8 reshape.6
  2.1 0.6 pad.9
  2.7 0.7 fusion.1
  3.4 0.6 broadcast_in_dim.10.pos
  4.1 1.2 copy.9
  5.3 0.8 pad.8.head_in
  6.1 155.2 %shard_map.82 = bf16[512,3840]{1,0:T(8,128)(2,1)} custom-call(bf16[256,1536]{1,0:T(8,128)(2,1)} %bitcast.6, bf16[512,1536]{1,0:T(8,128)(2,1)} %bitcast.5, f32[3,1536]{1,0:T(4,128)} %depth.1, bf16[48,1536]{1,0:T(8,128)(2,1)} %sep_in.1, bf16[1536,128]{1,0:T(8,128)(2,1)} %pad.8.head_in, f32[1,1536]{1,0:T(1,128)} %broadcast_in_dim.9.sep_b, f32[1,4096]{1,0:T(1,128)} %bitcast.7, ...), custom_call_target="tpu_custom_call" | custom-call | tf_op jit(solution)/shard_map/pallas_call | solution.py:363
  161.3 4.3 %copy.11 = bf16[1,512,3840]{2,1,0:T(8,128)(2,1)} copy(bf16[1,512,3840]{2,1,0:T(8,128)(2,1)} %bitcast.4) | data formatting | bytes 7864320

commit v4 on v3

--- a/solution.py
+++ b/solution.py
@@ -34,7 +34,7 @@
 
 
 def kernel(
-    coarse, skip, depth, sep_in, head_in, sep_b, head_b, pos,
+    coarse, skip, depth, sep_in, head_in, vectors,
     out,
     wsep, whead, merged, dw, rev, mirrored, feat, featm, hown, hpart, perm, stage,
     local_sem, halo_send, halo_recv, ex_send, ex_recv, z_send, z_recv, y_send, y_recv,
@@ -179,14 +179,14 @@
         @pl.loop(0, D // 256)
         def _(n):
             v = jnp.dot(block[...], wsep[:, tile(n)], preferred_element_type=jnp.float32)
-            dst[:, tile(n)] = gelu(v + sep_b[:, tile(n)]).astype(jnp.bfloat16)
+            dst[:, tile(n)] = gelu(v + vectors[:, tile(n)]).astype(jnp.bfloat16)
 
     def head(block, dst, rows, e):
         @pl.loop(0, 4)
         def _(k):
             j = slot(k, e)
             v = jnp.dot(block[...], whead[j], preferred_element_type=jnp.float32)
-            dst[rows, tile(j)] = softplus(v + head_b[:, tile(j)]).astype(jnp.bfloat16)
+            dst[rows, tile(j)] = softplus(v + vectors[:, tile(D // 256 + j)]).astype(jnp.bfloat16)
 
     locals_ = [
         pltpu.make_async_copy(own_view(p), view(p, slot(0, 0), c), local_sem.at[p]) for p in (0, 1)
@@ -245,7 +245,7 @@
         return jnp.where(row[:rows] == place, 1.0, 0.0).astype(jnp.bfloat16)
 
     def moved(rows, n, es):
-        source = pos[:, tile(n)]
+        source = vectors[:, tile(D // 256 + BLOCKS + n)].astype(jnp.int32)
         total = 0.0
         for e in es:
             for k in range(4):
@@ -357,13 +357,13 @@
                 s_copy(p, k, e).wait_send()
 
 
-def fused(coarse, skip, depth, sep_in, head_in, sep_b, head_b, pos):
+def fused(coarse, skip, depth, sep_in, head_in, vectors):
     dma = pltpu.SemaphoreType.DMA
     vmem = pl.BlockSpec(memory_space=pltpu.VMEM)
     return pl.pallas_call(
         kernel,
         out_shape=jax.ShapeDtypeStruct((ROWS, TRACKS), jnp.bfloat16),
-        in_specs=[vmem] * 8,
+        in_specs=[vmem] * 6,
         out_specs=pl.BlockSpec(memory_space=pl.ANY),
         scratch_shapes=[
             pltpu.VMEM((D, D), jnp.bfloat16),
@@ -396,7 +396,7 @@
         compiler_params=pltpu.CompilerParams(
             collective_id=0, has_side_effects=True, vmem_limit_bytes=60 * 1024 * 1024
         ),
-    )(coarse, skip, depth, sep_in, head_in, sep_b, head_b, pos)
+    )(coarse, skip, depth, sep_in, head_in, vectors)
 
 
 def per_device(
@@ -404,15 +404,14 @@
 ):
     pos = (strand_pair // SHARD) * LANES + strand_pair % SHARD
     bias = jnp.pad(head_bias.reshape(-1, SHARD), ((0, 0), (0, LANES - SHARD)))
+    vectors = jnp.concatenate([sep_bias, bias.reshape(-1), pos.astype(jnp.float32)])
     preds = fused(
         coarse[0],
         skip[0],
         depth_kernel,
         sep_weight,
         jnp.pad(head_weight, ((0, 0), (0, LANES - SHARD))),
-        sep_bias[None],
-        bias.reshape(1, -1),
-        pos[None],
+        vectors[None],
     )
     return preds[None]
 

time: 166 us -> 165 us (level)
  local copies, waits for them, and re-layouts: 9.63 us -> 7.77 us
where the time goes in v4:
time: 165 us; the launch traced here: 164 us
  Pallas kernels  155 us (94%)
  local copies, waits for them, and re-layouts  7.77 us (5%)
    pallas_call x1, Pallas kernels, fused(): pl.pallas_call(kernel, out_shape=jax.ShapeDtypeStruct((ROWS, TRACKS), jnp...  155 us
    unnamed x2, local copies, waits for them, and re-layouts  5.5 us

profile of v4, /device:TPU:1, one launch (start us, length us, event | category | flops | bytes accessed | tf_op | source)
XLA Modules:
  0.0 164.4 jit_solution(15491284470012412263)
XLA Ops:
  0.0 0.8 reshape.6
  0.8 0.7 fusion.2
  1.6 0.7 pad_maximum_fusion
  2.3 0.6 broadcast_in_dim.6.vectors
  2.9 1.2 copy.9
  4.1 0.8 pad.8.head_in
  5.0 155.2 %shard_map.82 = bf16[512,3840]{1,0:T(8,128)(2,1)} custom-call(bf16[256,1536]{1,0:T(8,128)(2,1)} %bitcast.7, bf16[512,1536]{1,0:T(8,128)(2,1)} %bitcast.6, f32[3,1536]{1,0:T(4,128)} %depth.1, bf16[48,1536]{1,0:T(8,128)(2,1)} %sep_in.1, bf16[1536,128]{1,0:T(8,128)(2,1)} %pad.8.head_in, f32[1,9472]{1,0:T(1,128)} %broadcast_in_dim.6.vectors), custom_call_target="tpu_custom_call" | custom-call | tf_op jit(solution)/shard_map/pallas_call | solution.py:363
  160.1 4.3 %copy.11 = bf16[1,512,3840]{2,1,0:T(8,128)(2,1)} copy(bf16[1,512,3840]{2,1,0:T(8,128)(2,1)} %bitcast.5) | data formatting | bytes 7864320
  (1 shorter events, 0.0 us)
